TPU v7x, 32 devices: a whole 2x2x4 slice. The times are simulated.
32 devices in a mesh: img: 2 (over core), pix: 16 (over z, y, x).
Axes of the slice: x: 2, y: 2, z: 4, core: 2. Of those that a mesh axis runs over, the one named last changes fastest.
Arguments:
- latents: bfloat16 [2, 256, 1024], P('img'), may hold values from -6 to 6
- pixels: float32 [2, 3, 6144], P('img', None, 'pix'), may hold values from -5 to 5
- coords: int32 [2, 2, 6144], P('img', None, 'pix'), may hold values from 0 to 223, as said below
- kept_mask: int32 [2, 6144], P('img', 'pix'), may hold values from 0 to 1, as said below
- lat_gain: float32 [1024], replicated, may hold values from 0.1 to 1.9
- lat_shift: float32 [1024], replicated, may hold values from -3 to 3
- query_weight: bfloat16 [1024, 1024], replicated, may hold values from -0.1875 to 0.1875
- query_bias: float32 [1024], replicated, may hold values from -3 to 3
- in_gain: float32 [261], replicated, may hold values from 0.1 to 1.9
- in_shift: float32 [261], replicated, may hold values from -3 to 3
- key_weight: bfloat16 [261, 1024], replicated, may hold values from -0.75 to 0.75
- value_weight: bfloat16 [261, 1024], replicated, may hold values from -2.023352 to 2.023352
- value_bias: float32 [1024], replicated, may hold values from -4 to 4
- mlp_gain: float32 [1024], replicated, may hold values from 0.1 to 1.9
- mlp_shift: float32 [1024], replicated, may hold values from -3 to 3
- up_weight: bfloat16 [1024, 1024], replicated, may hold values from -0.1875 to 0.1875
- up_bias: float32 [1024], replicated, may hold values from -3 to 3
- down_weight: bfloat16 [1024, 1024], replicated, may hold values from -0.1875 to 0.1875
- down_bias: float32 [1024], replicated, may hold values from -3 to 3
- cotangent: bfloat16 [2, 256, 1024], P('img'), may hold values from -6 to 6
Outputs:
- encoded: bfloat16 [2, 256, 1024], P('img')
- latent_grad: float32 [2, 256, 1024], P('img')
- pixel_grad: float32 [2, 3, 6144], P('img', None, 'pix')
- lat_gain_grad: float32 [1024], replicated
- lat_shift_grad: float32 [1024], replicated
- query_weight_grad: float32 [1024, 1024], replicated
- query_bias_grad: float32 [1024], replicated
- in_gain_grad: float32 [261], replicated
- in_shift_grad: float32 [261], replicated
- key_weight_grad: float32 [261, 1024], replicated
- value_weight_grad: float32 [261, 1024], replicated
- value_bias_grad: float32 [1024], replicated
- mlp_gain_grad: float32 [1024], replicated
- mlp_shift_grad: float32 [1024], replicated
- up_weight_grad: float32 [1024, 1024], replicated
- up_bias_grad: float32 [1024], replicated
- down_weight_grad: float32 [1024, 1024], replicated
- down_bias_grad: float32 [1024], replicated
Inputs may be any that keep to these rules, and one draw needn't show every extreme that they name: `coords`: for each image the pixels are distinct cells of a 224 x 224 grid in row-major order, given as (row, column); the first and the last cell of the grid are always among them. `kept_mask`: exactly half of each image's pixels are kept; dropped keys cluster in square patches of 16 x 16 grid cells, with a share that varies by patch row.
All inputs are finite; a program needn't handle non-finite values.
Results may differ from a plain program's by a relative error of at most 0.017.
The roundings to bfloat16 on the way count: a program that leaves them out, or rounds other values in their place, can miss the bound.
Values may be sent and summed in bfloat16 or wider, within the bound.
No kernel may reach another device: no remote copies, remote signals or barrier semaphores. Data moves between devices by JAX's collectives and lax.ppermute only.
A program may use at most 128 MiB of HBM per device.

v0:
```python
from functools import partial
import math
import jax
import jax.numpy as jnp
from jax import lax
from jax.sharding import PartitionSpec as P

BANDS = 64
GRID = 224
EPSILON = 1e-05
HIGHEST = lax.Precision.HIGHEST
FLOOR = -1e30


def norm_axis(values, gain_vec, shift_vec, axis_pos):
    centre = values - jnp.mean(values, axis=axis_pos, keepdims=True)
    spread_sq = jnp.mean(centre * centre, axis=axis_pos, keepdims=True)
    return centre * lax.rsqrt(spread_sq + EPSILON) * gain_vec + shift_vec


def fourier_table(colors, grid_pos):
    position = grid_pos.astype(jnp.float32) * (2.0 / (GRID - 1)) - 1.0
    frequency = 1.0 + jnp.arange(BANDS, dtype=jnp.float32) * ((GRID / 2.0 - 1.0) / (BANDS - 1))
    phases = (position[:, None, :] * (math.pi * frequency)[None, :, None]).reshape(
        2 * BANDS, position.shape[1]
    )
    return jnp.concatenate([colors, position, jnp.sin(phases), jnp.cos(phases)], axis=0)


def contract(left, right, left_dim, right_dim, exact=None):
    return lax.dot_general(
        left,
        right,
        (((left_dim,), (right_dim,)), ((), ())),
        precision=exact,
        preferred_element_type=jnp.float32,
    )


def forward_pass(latents, pixels, coords, kept_mask, weights):
    (
        lat_gain,
        lat_shift,
        query_weight,
        query_bias,
        in_gain,
        in_shift,
        key_weight,
        value_weight,
        value_bias,
        mlp_gain,
        mlp_shift,
        up_weight,
        up_bias,
        down_weight,
        down_bias,
    ) = weights
    latent = latents[0].astype(jnp.float32)
    norm_one = norm_axis(latent, lat_gain, lat_shift, 1).astype(jnp.bfloat16)
    query = (
        jnp.dot(norm_one, query_weight, preferred_element_type=jnp.float32) + query_bias
    ).astype(jnp.bfloat16)
    table = fourier_table(pixels[0], coords[0]).astype(jnp.bfloat16)
    live_row = kept_mask[0].astype(jnp.bfloat16)
    slot_order = jnp.arange(live_row.shape[0], dtype=jnp.int32)
    table_full = table.astype(jnp.float32)
    x_in = norm_axis(table_full, in_gain[:, None], in_shift[:, None], 0).astype(jnp.bfloat16)
    keys = contract(x_in, key_weight, 0, 0).astype(jnp.bfloat16)
    values = (contract(x_in, value_weight, 0, 0) + value_bias).astype(jnp.bfloat16)
    inv_root = 1.0 / math.sqrt(query.shape[1])
    score = contract(query, keys, 1, 1) * inv_root
    live_mask = live_row > 0
    local_top = jnp.max(jnp.where(live_mask, score, FLOOR), axis=1)
    values_full = values.astype(jnp.float32)
    row_top = lax.pmax(local_top, "pix")
    weight = jnp.where(live_mask, jnp.exp(score - row_top[:, None]), 0.0)
    row_total, weighted = lax.psum(
        (jnp.sum(weight, axis=1), jnp.dot(weight, values_full, precision=HIGHEST)), "pix"
    )
    attn = weighted / row_total[:, None]
    mixed = latent + attn
    norm_two = norm_axis(mixed, mlp_gain, mlp_shift, 1).astype(jnp.bfloat16)
    pre_act = jnp.dot(norm_two, up_weight, preferred_element_type=jnp.float32) + up_bias
    hidden = jax.nn.gelu(pre_act, approximate=False).astype(jnp.bfloat16)
    encoded = mixed + jnp.dot(hidden, down_weight, preferred_element_type=jnp.float32) + down_bias
    saved = (
        latent,
        norm_one,
        query,
        table_full,
        x_in,
        keys,
        values,
        score,
        live_mask,
        row_top,
        row_total,
        attn,
        mixed,
        norm_two,
        pre_act,
        hidden,
        slot_order,
        slot_order,
    )
    return (encoded.astype(jnp.bfloat16)[None], saved)


def shards(
    latents,
    pixels,
    coords,
    kept_mask,
    lat_gain,
    lat_shift,
    query_weight,
    query_bias,
    in_gain,
    in_shift,
    key_weight,
    value_weight,
    value_bias,
    mlp_gain,
    mlp_shift,
    up_weight,
    up_bias,
    down_weight,
    down_bias,
    cotangent,
):
    weights = (
        lat_gain,
        lat_shift,
        query_weight,
        query_bias,
        in_gain,
        in_shift,
        key_weight,
        value_weight,
        value_bias,
        mlp_gain,
        mlp_shift,
        up_weight,
        up_bias,
        down_weight,
        down_bias,
    )
    encoded, saved = forward_pass(latents, pixels, coords, kept_mask, weights)
    fresh = lax.optimization_barrier((latents, pixels, coords, kept_mask, weights))
    discarded, saved = forward_pass(fresh[0], fresh[1], fresh[2], fresh[3], fresh[4])
    (
        latent,
        norm_one,
        query,
        table_full,
        x_in,
        keys,
        values,
        score,
        live_mask,
        row_top,
        row_total,
        attn,
        mixed,
        norm_two,
        pre_act,
        hidden,
        slot_order,
        kept_index,
    ) = saved
    inv_root = 1.0 / math.sqrt(query.shape[1])
    out_grad = cotangent[0]
    out_grad_full = out_grad.astype(jnp.float32)
    down_weight_grad = contract(hidden, out_grad, 0, 0)
    down_bias_grad = jnp.sum(out_grad_full, axis=0)
    hidden_grad = contract(out_grad, down_weight, 1, 1)
    ignored, gelu_pull = jax.vjp(partial(jax.nn.gelu, approximate=False), pre_act)
    pre_grad = gelu_pull(hidden_grad)[0].astype(jnp.bfloat16)
    up_weight_grad = contract(norm_two, pre_grad, 0, 0)
    up_bias_grad = jnp.sum(pre_grad.astype(jnp.float32), axis=0)
    norm_two_grad = contract(pre_grad, up_weight, 1, 1)
    ignored, mlp_pull = jax.vjp(partial(norm_axis, axis_pos=1), mixed, mlp_gain, mlp_shift)
    mixed_part, mlp_gain_grad, mlp_shift_grad = mlp_pull(norm_two_grad)
    mixed_grad = out_grad_full + mixed_part
    attn_grad = mixed_grad.astype(jnp.bfloat16)
    attn_grad_full = attn_grad.astype(jnp.float32)
    row_delta = jnp.sum(attn_grad_full * attn, axis=1)
    prob = jnp.where(live_mask, jnp.exp(score - row_top[:, None]), 0.0) / row_total[:, None]
    prob_grad = contract(attn_grad, values, 1, 1)
    score_grad = (prob * (prob_grad - row_delta[:, None])).astype(jnp.bfloat16)
    query_part = jnp.dot(score_grad, keys, preferred_element_type=jnp.float32) * inv_root
    key_grad = (contract(score_grad, query, 0, 0) * inv_root).astype(jnp.bfloat16)
    value_grad = contract(prob, attn_grad_full, 0, 0, HIGHEST).astype(jnp.bfloat16)
    key_weight_grad = contract(x_in, key_grad, 1, 0)
    value_weight_grad = contract(x_in, value_grad, 1, 0)
    value_bias_grad = jnp.sum(value_grad.astype(jnp.float32), axis=0)
    x_in_grad = contract(key_weight, key_grad, 1, 1) + contract(value_weight, value_grad, 1, 1)
    ignored, input_pull = jax.vjp(
        partial(norm_axis, axis_pos=0), table_full, in_gain[:, None], in_shift[:, None]
    )
    table_grad, in_gain_col, in_shift_col = input_pull(x_in_grad)
    color_grad = table_grad[:3]
    query_grad = lax.psum(query_part, "pix").astype(jnp.bfloat16)
    query_weight_grad = contract(norm_one, query_grad, 0, 0)
    query_bias_grad = jnp.sum(query_grad.astype(jnp.float32), axis=0)
    norm_one_grad = contract(query_grad, query_weight, 1, 1)
    ignored, latent_pull = jax.vjp(partial(norm_axis, axis_pos=1), latent, lat_gain, lat_shift)
    latent_part, lat_gain_grad, lat_shift_grad = latent_pull(norm_one_grad)
    latent_grad = mixed_grad + latent_part
    pixel_sums = lax.psum(
        (
            key_weight_grad,
            value_weight_grad,
            value_bias_grad,
            in_gain_col[:, 0],
            in_shift_col[:, 0],
        ),
        ("img", "pix"),
    )
    replica_sums = (
        lax.psum(lat_gain_grad.astype(jnp.bfloat16), "img").astype(jnp.float32),
        lax.psum(lat_shift_grad.astype(jnp.bfloat16), "img").astype(jnp.float32),
        lax.psum(query_weight_grad.astype(jnp.bfloat16), "img").astype(jnp.float32),
        lax.psum(query_bias_grad.astype(jnp.bfloat16), "img").astype(jnp.float32),
        lax.psum(mlp_gain_grad.astype(jnp.bfloat16), "img").astype(jnp.float32),
        lax.psum(mlp_shift_grad.astype(jnp.bfloat16), "img").astype(jnp.float32),
        lax.psum(up_weight_grad.astype(jnp.bfloat16), "img").astype(jnp.float32),
        lax.psum(up_bias_grad.astype(jnp.bfloat16), "img").astype(jnp.float32),
        lax.psum(down_weight_grad.astype(jnp.bfloat16), "img").astype(jnp.float32),
        lax.psum(down_bias_grad.astype(jnp.bfloat16), "img").astype(jnp.float32),
    )
    return (
        encoded,
        latent_grad[None],
        color_grad[None],
        replica_sums[0],
        replica_sums[1],
        replica_sums[2],
        replica_sums[3],
        pixel_sums[3],
        pixel_sums[4],
        pixel_sums[0],
        pixel_sums[1],
        pixel_sums[2],
        replica_sums[4],
        replica_sums[5],
        replica_sums[6],
        replica_sums[7],
        replica_sums[8],
        replica_sums[9],
    )


def solution(mesh):
    return jax.shard_map(
        shards,
        mesh=mesh,
        in_specs=(
            P("img", None, None),
            P("img", None, "pix"),
            P("img", None, "pix"),
            P("img", "pix"),
            P(),
            P(),
            P(),
            P(),
            P(),
            P(),
            P(),
            P(),
            P(),
            P(),
            P(),
            P(),
            P(),
            P(),
            P(),
            P("img", None, None),
        ),
        out_specs=(
            P("img", None, None),
            P("img", None, None),
            P("img", None, "pix"),
            P(),
            P(),
            P(),
            P(),
            P(),
            P(),
            P(),
            P(),
            P(),
            P(),
            P(),
            P(),
            P(),
            P(),
            P(),
        ),
        check_vma=False,
    )
```

profile of v0, /device:TPU:0, one launch (start us, length us, event | category | flops | bytes accessed | tf_op | source)
XLA Modules:
  0.0 493.2 jit_solution(3824822552677520739)
XLA Ops:
  14.1 2.8 add_convert_fusion.1
  20.1 3.0 select_reduce_fusion.1
  23.1 1.9 convolution_convert_fusion.3
  26.7 43.5 %all-reduce.4 = (f32[256]{0:T(256)S(1)}, f32[256]{0:T(256)S(1)}) all-reduce(f32[256]{0:T(256)S(1)} %get-tuple-element.120, f32[256]{0:T(256)S(1)} %get-tuple-element.122), channel_id=1, replica_groups=mesh['img'=2,'pix'=16] {'pix'}, use_global_device_ids=true, to_apply=%region_5.6 | all-reduce | flops 512 | bytes 4096 | tf_op jit(solution)/shard_map/pmax | solution.py:75
  70.2 1.9 add_convert_fusion
  72.1 2.0 fusion.115
  74.1 2.0 fusion.118
  76.5 37.6 %psum.143 = f32[256]{0:T(256)S(1)} all-reduce(f32[256]{0:T(256)S(1)} %fusion.117), channel_id=1, replica_groups=mesh['img'=2,'pix'=16] {'pix'}, use_global_device_ids=true, to_apply=%region_19.20 | all-reduce | flops 256 | bytes 2048 | tf_op jit(solution)/shard_map/psum | solution.py:77
  115.8 83.1 %all-reduce.14.cloned.1.call-done = (f32[256,1024]{1,0:T(8,128)}, f32[256,1024]{1,0:T(8,128)}) async-done(((f32[256,1024]{1,0:T(8,128)}, f32[256,1024]{1,0:T(8,128)}), (f32[256,1024]{1,0:T(8,128)}, f32[256,1024]{1,0:T(8,128)})) %all-reduce.14.cloned.1.call-update) | async-done | bytes 2097168 | tf_op jit(solution)/shard_map/psum | solution.py:77
  202.5 3.7 fusion.201
  207.9 2.2 convolution_convert_fusion.1
  210.1 4.0 convolution_convert_fusion
  218.8 89.6 %all-reduce.17 = (f32[256]{0:T(256)}, bf16[256,1024]{1,0:T(8,128)(2,1)}) all-reduce(f32[256]{0:T(256)} %fusion.114, f32[256,1024]{1,0:T(8,128)} %convolution_multiply_fusion), channel_id=1, replica_groups=mesh['img'=2,'pix'=16] {'pix'}, use_global_device_ids=true, to_apply=%region_8.9 | all-reduce | flops 262400 | bytes 1574912 | tf_op jit(solution)/shard_map/psum | solution.py:77
  308.4 3.3 convolution_convert_fusion.2
  315.8 2.2 fusion.191
  326.2 3.0 add_bitcast_fusion
  330.9 3.3 all-reduce.5
  338.6 37.2 %all-reduce = (f32[261]{0:T(512)}, f32[261]{0:T(512)}, f32[1024]{0:T(1024)}) all-reduce(f32[261]{0:T(512)S(1)} %get-tuple-element.77, f32[261]{0:T(512)S(1)} %reduce_sum.377, f32[1024]{0:T(1024)S(1)} %get-tuple-element.129), channel_id=1, replica_groups=mesh['img'=2,'pix'=16] {'img','pix'}, use_global_device_ids=true, to_apply=%region_38.39 | all-reduce | flops 1546 | bytes 12368 | tf_op jit(solution)/shard_map/psum | solution.py:210
  375.8 6.7 %fusion.15 = bf16[1,256,1024]{2,1,0:T(8,128)(2,1)} fusion(f32[256,1024]{1,0:T(8,128)} %copy-done.6, bf16[1024,1024]{1,0:T(8,128)(2,1)} %param.37, bf16[1024,1024]{1,0:T(8,128)(2,1)S(1)} %copy-done, f32[1024]{0:T(1024)S(1)} %copy-done.82, f32[1024]{0:T(1024)S(1)} %copy-done.81, f32[1024]{0:T(1024)S(1)} %copy-done.60, f32[1024]{0:T(1024)S(1)} %copy-done.36, ...), kind=kOutput, calls=%fused_computation.39 | convolution fusion | flops 1093140480 | bytes 5785600 | tf_op jit(solution)/shard_map/dot_general | solution.py:85
  382.5 4.2 convert_element_type.211
  386.7 2.5 convert_element_type.219
  389.2 2.5 convert_element_type.223
  391.7 91.6 %all-reduce.12.cloned.1.call-done = (f32[261,1024]{1,0:T(8,128)}, f32[261,1024]{1,0:T(8,128)}) async-done(((f32[261,1024]{1,0:T(8,128)}, f32[261,1024]{1,0:T(8,128)}), (f32[261,1024]{1,0:T(8,128)}, f32[261,1024]{1,0:T(8,128)})) %all-reduce.12.cloned.1.call-update) | async-done | bytes 2138128 | tf_op jit(solution)/shard_map/psum | solution.py:210
  483.3 2.4 copy.59
  (244 shorter events, 42.1 us)
Async XLA Ops:
  7.2 193.5 %copy-start = (bf16[1024,1024]{1,0:T(8,128)(2,1)S(1)}, bf16[1024,1024]{1,0:T(8,128)(2,1)}, u32[]{:S(2)}) copy-start(bf16[1024,1024]{1,0:T(8,128)(2,1)} %param.35) | copy-start | bytes 6291460
  7.2 191.7 %all-reduce.14.cloned.1.call-start = ((), (), s32[]{:S(2)}) async-start(), calls=%async_computation.1 | async-start | bytes 4194304 | tf_op jit(solution)/shard_map/psum | solution.py:77
  9.5 7.5 %copy-start.1 = (bf16[1,256,1024]{2,1,0:T(8,128)(2,1)S(1)}, bf16[1,256,1024]{2,1,0:T(8,128)(2,1)}, u32[]{:S(2)}) copy-start(bf16[1,256,1024]{2,1,0:T(8,128)(2,1)} %param.20) | copy-start | bytes 1572868
  18.9 57.3 %copy-start.56 = (pred[384]{0:T(512)(128)(4,1)}, pred[384]{0:T(512)(128)(4,1)S(1)}, u32[]{:S(2)}) copy-start(pred[384]{0:T(512)(128)(4,1)S(1)} %compare_reduce_fusion) | copy-start | bytes 1156
  19.1 5.9 %copy-start.37 = (f32[256]{0:T(256)}, f32[256]{0:T(256)S(1)}, u32[]{:S(2)}) copy-start(f32[256]{0:T(256)S(1)} %broadcast_multiply_fusion.3) | copy-start | bytes 3076
  19.4 5.6 %copy-start.46 = (f32[256]{0:T(256)}, f32[256]{0:T(256)S(1)}, u32[]{:S(2)}) copy-start(f32[256]{0:T(256)S(1)} %fusion.137) | copy-start | bytes 3076
  20.1 4.9 %copy-start.30 = (f32[384]{0:T(512)}, f32[384]{0:T(512)S(1)}, u32[]{:S(2)}) copy-start(f32[384]{0:T(512)S(1)} %fusion.112) | copy-start | bytes 4612
  25.0 45.1 %copy-start.78 = (f32[1024]{0:T(1024)S(1)}, f32[1024]{0:T(1024)}, u32[]{:S(2)}) copy-start(f32[1024]{0:T(1024)} %param.32) | copy-start | bytes 12292
  26.7 49.5 %copy-start.11 = (f32[256,384]{1,0:T(8,128)}, f32[256,384]{1,0:T(8,128)S(1)}, u32[]{:S(2)}) copy-start(f32[256,384]{1,0:T(8,128)S(1)} %get-tuple-element.123) | copy-start | bytes 1179652
  70.2 6.0 %copy-start.61 = (f32[256]{0:T(256)}, f32[256]{0:T(256)S(1)}, u32[]{:S(2)}) copy-start(f32[256]{0:T(256)S(1)} %get-tuple-element.89) | copy-start | bytes 3076
  76.1 306.4 %all-reduce.16.cloned.1.call-start = ((), (), s32[]{:S(2)}) async-start(), calls=%async_computation.2 | async-start | bytes 12582912 | tf_op jit(solution)/shard_map/psum | solution.py:223
  76.4 124.3 %copy-start.35 = (f32[1024]{0:T(1024)S(1)}, f32[1024]{0:T(1024)}, u32[]{:S(2)}) copy-start(f32[1024]{0:T(1024)} %param.33) | copy-start | bytes 12292
  76.4 124.3 %copy-start.59 = (f32[1024]{0:T(1024)S(1)}, f32[1024]{0:T(1024)}, u32[]{:S(2)}) copy-start(f32[1024]{0:T(1024)} %param.34) | copy-start | bytes 12292
  76.5 124.3 %copy-start.80 = (f32[1024]{0:T(1024)S(1)}, f32[1024]{0:T(1024)}, u32[]{:S(2)}) copy-start(f32[1024]{0:T(1024)} %param.36) | copy-start | bytes 12292
  114.0 100.6 %copy-start.40 = (f32[256]{0:T(256)}, f32[256]{0:T(256)S(1)}, u32[]{:S(2)}) copy-start(f32[256]{0:T(256)S(1)} %psum.143) | copy-start | bytes 3076
  311.8 171.5 %all-reduce.12.cloned.1.call-start = ((), (), s32[]{:S(2)}) async-start(), calls=%async_computation | async-start | bytes 4325376 | tf_op jit(solution)/shard_map/psum | solution.py:210
  315.8 4.5 copy-start.23
  329.2 6.8 %copy-start.10 = (f32[384,261]{0,1:T(8,128)S(1)}, f32[384,261]{0,1:T(8,128)}, u32[]{:S(2)}) copy-start(f32[384,261]{0,1:T(8,128)} %copy-done.9) | copy-start | bytes 1202692
  329.2 46.6 %copy-start.36 = (f32[1024]{0:T(1024)S(1)}, f32[1024]{0:T(1024)}, u32[]{:S(2)}) copy-start(f32[1024]{0:T(1024)} %param.33) | copy-start | bytes 12292
  329.2 46.6 %copy-start.60 = (f32[1024]{0:T(1024)S(1)}, f32[1024]{0:T(1024)}, u32[]{:S(2)}) copy-start(f32[1024]{0:T(1024)} %param.34) | copy-start | bytes 12292
  329.2 46.5 %copy-start.66 = (f32[256]{0:T(256)S(1)}, f32[256]{0:T(256)}, u32[]{:S(2)}) copy-start(f32[256]{0:T(256)} %copy-done.65) | copy-start | bytes 3076
  329.2 46.5 %copy-start.71 = (f32[256]{0:T(256)S(1)}, f32[256]{0:T(256)}, u32[]{:S(2)}) copy-start(f32[256]{0:T(256)} %add_rsqrt_fusion.1) | copy-start | bytes 3076
  329.3 46.5 %copy-start.81 = (f32[1024]{0:T(1024)S(1)}, f32[1024]{0:T(1024)}, u32[]{:S(2)}) copy-start(f32[1024]{0:T(1024)} %param.36) | copy-start | bytes 12292
  329.3 46.5 %copy-start.82 = (f32[1024]{0:T(1024)S(1)}, f32[1024]{0:T(1024)}, u32[]{:S(2)}) copy-start(f32[1024]{0:T(1024)} %param.38) | copy-start | bytes 12292
  (62 other events, 134.3 us)
Sparse Core Ops, SparseCore 0:
  76.3 122.6 all-reduce.13
  311.9 28.9 all-reduce.15
  347.3 135.9 all-reduce.11
where the time goes:
time: 494 us; the launch traced here: 493 us
  blocking collectives  211 us (43%)
  waiting for transfers between devices  175 us (35%)
  matrix products  49 us (10%)
  other arithmetic  32.3 us (7%)
  between operations  14.9 us (3%)
  local copies, waits for them, and re-layouts  10.8 us (2%)
    psum x2, blocking collectives, forward_pass(): lax.psum((jnp.sum(weight, axis=1), jnp.dot(weight, values_full, precision...  127 us
    psum x1, waiting for transfers between devices, shards(): lax.psum((key_weight_grad, value_weight_grad, value_bias_grad, in_gain_co...  91.6 us
    psum x1, waiting for transfers between devices, forward_pass(): lax.psum((jnp.sum(weight, axis=1), jnp.dot(weight, values_full, precision...  83.1 us
    pmax x1, blocking collectives, forward_pass(): row_top = lax.pmax(local_top, 'pix')  43.5 us
    psum x1, blocking collectives, shards(): lax.psum((key_weight_grad, value_weight_grad, value_bias_grad, in_gain_co...  37.2 us
    dot_general x18, matrix products, contract(): lax.dot_general(left, right, (((left_dim,), (right_dim,)), ((), ())), pre...  33.8 us
    unnamed x170, local copies, waits for them, and re-layouts  10.1 us
  transfers between devices with their start and end apart: 3, of which 2 were waited for; matrix products, arithmetic and copies ran while one was open for 8% of the time, Pallas kernels for 0%

commit v1 on v0

--- a/solution.py
+++ b/solution.py
@@ -208,14 +208,17 @@
     latent_part, lat_gain_grad, lat_shift_grad = latent_pull(norm_one_grad)
     latent_grad = mixed_grad + latent_part
     pixel_sums = lax.psum(
-        (
-            key_weight_grad,
-            value_weight_grad,
-            value_bias_grad,
-            in_gain_col[:, 0],
-            in_shift_col[:, 0],
+        lax.psum(
+            (
+                key_weight_grad,
+                value_weight_grad,
+                value_bias_grad,
+                in_gain_col[:, 0],
+                in_shift_col[:, 0],
+            ),
+            "pix",
         ),
-        ("img", "pix"),
+        "img",
     )
     replica_sums = (
         lax.psum(lat_gain_grad.astype(jnp.bfloat16), "img").astype(jnp.float32),

time: 494 us -> 430 us (0.87)
  waiting for transfers between devices: 175 us -> 132 us
  blocking collectives: 211 us -> 185 us
    psum x1, waiting for transfers between devices: 91.6 us -> 15.8 us  [shards(): lax.psum(lax.psum((key_weight_grad, value_weight_grad, value_bias_grad, i...]
    psum x1, blocking collectives: 37.2 us -> 3.06 us  [shards(): lax.psum(lax.psum((key_weight_grad, value_weight_grad, value_bias_grad, i...]
    psum x1, waiting for transfers between devices: 0.01 us -> 24.5 us  [shards(): lax.psum(query_weight_grad.astype(jnp.bfloat16), 'img').astype(jnp.float32)]
    psum x1 -> x2, waiting for transfers between devices: 83.1 us -> 92 us  [forward_pass(): lax.psum((jnp.sum(weight, axis=1), jnp.dot(weight, values_full, precision...]
    psum x2, blocking collectives: 127 us -> 136 us  [forward_pass(): lax.psum((jnp.sum(weight, axis=1), jnp.dot(weight, values_full, precision...]
    unnamed x170 -> x132, local copies, waits for them, and re-layouts: 10.1 us -> 11.9 us
  transfers between devices with their start and end apart: 3 -> 4, of which waited for: 2 -> 4; matrix products, arithmetic and copies ran while one was open for 8% -> 12% of each run, Pallas kernels for 0% -> 0%
where the time goes in v1:
time: 430 us; the launch traced here: 429 us
  blocking collectives  185 us (43%)
  waiting for transfers between devices  132 us (31%)
  matrix products  51 us (12%)
  other arithmetic  33 us (8%)
  between operations  14.6 us (3%)
  local copies, waits for them, and re-layouts  12.7 us (3%)
    psum x2, blocking collectives, forward_pass(): lax.psum((jnp.sum(weight, axis=1), jnp.dot(weight, values_full, precision...  136 us
    psum x2, waiting for transfers between devices, forward_pass(): lax.psum((jnp.sum(weight, axis=1), jnp.dot(weight, values_full, precision...  92 us
    pmax x1, blocking collectives, forward_pass(): row_top = lax.pmax(local_top, 'pix')  43.5 us
    dot_general x18, matrix products, contract(): lax.dot_general(left, right, (((left_dim,), (right_dim,)), ((), ())), pre...  33.1 us
    psum x1, waiting for transfers between devices, shards(): lax.psum(query_weight_grad.astype(jnp.bfloat16), 'img').astype(jnp.float32)  24.5 us
    psum x1, waiting for transfers between devices, shards(): lax.psum(lax.psum((key_weight_grad, value_weight_grad, value_bias_grad, i...  15.8 us
    unnamed x132, local copies, waits for them, and re-layouts  11.9 us
  transfers between devices with their start and end apart: 4, of which 4 were waited for; matrix products, arithmetic and copies ran while one was open for 12% of the time, Pallas kernels for 0%

profile of v1, /device:TPU:0, one launch (start us, length us, event | category | flops | bytes accessed | tf_op | source)
XLA Modules:
  0.0 429.3 jit_solution(7070723672133240074)
XLA Ops:
  15.5 3.2 fusion.10
  19.8 2.3 select_reduce_fusion.1
  26.3 43.5 %all-reduce.2 = (f32[256]{0:T(256)S(1)}, f32[256]{0:T(256)S(1)}) all-reduce(f32[256]{0:T(256)S(1)} %get-tuple-element.124, f32[256]{0:T(256)S(1)} %get-tuple-element.126), channel_id=1, replica_groups=mesh['img'=2,'pix'=16] {'pix'}, use_global_device_ids=true, to_apply=%region_5.6 | all-reduce | flops 512 | bytes 4096 | tf_op jit(solution)/shard_map/pmax | solution.py:75
  75.8 37.0 %psum.178 = f32[256]{0:T(256)S(1)} all-reduce(f32[256]{0:T(256)S(1)} %fusion.117), channel_id=1, replica_groups=mesh['img'=2,'pix'=16] {'pix'}, use_global_device_ids=true, to_apply=%region_19.20 | all-reduce | flops 256 | bytes 2048 | tf_op jit(solution)/shard_map/psum | solution.py:77
  114.6 2.0 fusion.115
  116.6 65.7 %all-reduce.13.cloned.1.call-done = f32[256,1024]{1,0:T(8,128)} async-done(((f32[256,1024]{1,0:T(8,128)}), f32[256,1024]{1,0:T(8,128)}) %all-reduce.13.cloned.1.call-update) | async-done | bytes 1048592 | tf_op jit(solution)/shard_map/psum | solution.py:77
  186.0 3.7 fusion.201
  201.4 2.7 convolution_multiply_fusion
  205.4 98.6 %all-reduce.20 = (f32[256]{0:T(256)S(1)}, bf16[256,1024]{1,0:T(8,128)(2,1)}, f32[261]{0:T(512)S(1)}, f32[261]{0:T(512)S(1)}, f32[1024]{0:T(1024)S(1)}) all-reduce(f32[256]{0:T(256)S(1)} %copy-done.48, f32[256,1024]{1,0:T(8,128)} %convolution_multiply_fusion, f32[261]{0:T(512)S(1)} %get-tuple-element.77, ...), channel_id=1, replica_groups=mesh['img'=2,'pix'=16] {'pix'}, use_global_device_ids=true, to_apply=%region_8.9 | all-reduce | flops 263946 | bytes 1587280 | tf_op jit(solution)/shard_map/psum | solution.py:77
  304.0 3.4 convolution_convert_fusion.2
  307.4 2.2 convolution_convert_fusion.1
  309.6 4.0 convolution_convert_fusion
  317.5 2.7 fusion.191
  321.8 3.3 all-reduce.5
  329.3 3.1 all-reduce.3
  332.3 26.3 %all-reduce.15.cloned.1.call-done = (f32[256,1024]{1,0:T(8,128)}, f32[261,1024]{1,0:T(8,128)}, f32[261,1024]{1,0:T(8,128)}) async-done(((f32[256,1024]{1,0:T(8,128)}, f32[261,1024]{1,0:T(8,128)}, f32[261,1024]{1,0:T(8,128)}), (f32[256,1024]{1,0:T(8,128)}, f32[261,1024]{1,0:T(8,128)}, f32[261,1024]{1,0:T(8,128)})) %all-reduce.15.cloned.1.call-update) | async-done | bytes 3186704 | tf_op jit(solution)/shard_map/psum | solution.py:77
  358.7 3.1 add_bitcast_fusion
  363.3 6.5 %fusion.15 = bf16[1,256,1024]{2,1,0:T(8,128)(2,1)} fusion(f32[256,1024]{1,0:T(8,128)} %copy-done.9, bf16[1024,1024]{1,0:T(8,128)(2,1)} %param.37, bf16[1024,1024]{1,0:T(8,128)(2,1)S(1)} %copy-done, f32[1024]{0:T(1024)S(1)} %copy-done.61, f32[1024]{0:T(1024)S(1)} %copy-done.60, f32[1024]{0:T(1024)S(1)} %copy-done.45, f32[1024]{0:T(1024)S(1)} %copy-done.35, ...), kind=kOutput, calls=%fused_computation.39 | convolution fusion | flops 1093140480 | bytes 5785600 | tf_op jit(solution)/shard_map/dot_general | solution.py:85
  369.9 24.5 %all-reduce.19.cloned.1.call-done = (bf16[1024,1024]{1,0:T(8,128)(2,1)}, bf16[1024,1024]{1,0:T(8,128)(2,1)}, bf16[1024,1024]{1,0:T(8,128)(2,1)}) async-done(((bf16[1024,1024]{1,0:T(8,128)(2,1)}, bf16[1024,1024]{1,0:T(8,128)(2,1)}, bf16[1024,1024]{1,0:T(8,128)(2,1)}), (bf16[1024,1024]{1,0:T(8,128)(2,1)}, bf16[1024,1024]{1,0:T(8,128)(2,1)}, bf16[1024,1024]{1,0:T(8,128)(2,1)})) %all-reduce.19.cloned.1.call-update) | async-done | bytes 6291472 | tf_op jit(solution)/shard_map/psum | solution.py:226
  394.4 4.2 convert_element_type.211
  398.6 2.5 convert_element_type.219
  401.1 2.5 convert_element_type.223
  403.6 15.8 %all-reduce.17.cloned.1.call-done = (f32[261,1024]{1,0:T(8,128)}, f32[261,1024]{1,0:T(8,128)}) async-done(((f32[261,1024]{1,0:T(8,128)}, f32[261,1024]{1,0:T(8,128)}), (f32[261,1024]{1,0:T(8,128)}, f32[261,1024]{1,0:T(8,128)})) %all-reduce.17.cloned.1.call-update) | async-done | bytes 2138128 | tf_op jit(solution)/shard_map/psum | solution.py:210
  419.3 2.4 copy.64
  (209 shorter events, 49.6 us)
Async XLA Ops:
  7.2 176.9 %copy-start = (bf16[1024,1024]{1,0:T(8,128)(2,1)S(1)}, bf16[1024,1024]{1,0:T(8,128)(2,1)}, u32[]{:S(2)}) copy-start(bf16[1024,1024]{1,0:T(8,128)(2,1)} %param.35) | copy-start | bytes 6291460
  7.2 8.2 %copy-start.1 = (bf16[1,256,1024]{2,1,0:T(8,128)(2,1)S(1)}, bf16[1,256,1024]{2,1,0:T(8,128)(2,1)}, u32[]{:S(2)}) copy-start(bf16[1,256,1024]{2,1,0:T(8,128)(2,1)} %param.20) | copy-start | bytes 1572868
  7.2 8.2 %copy-start.34 = (f32[1024]{0:T(1024)S(1)}, f32[1024]{0:T(1024)}, u32[]{:S(2)}) copy-start(f32[1024]{0:T(1024)} %param.24) | copy-start | bytes 12292
  7.2 8.2 %copy-start.57 = (f32[1024]{0:T(1024)S(1)}, f32[1024]{0:T(1024)}, u32[]{:S(2)}) copy-start(f32[1024]{0:T(1024)} %param.25) | copy-start | bytes 12292
  7.2 8.2 %copy-start.55 = (f32[1024]{0:T(1024)S(1)}, f32[1024]{0:T(1024)}, u32[]{:S(2)}) copy-start(f32[1024]{0:T(1024)} %param.27) | copy-start | bytes 12292
  7.2 175.1 %all-reduce.13.cloned.1.call-start = ((), (), s32[]{:S(2)}) async-start(), calls=%async_computation | async-start | bytes 2097152 | tf_op jit(solution)/shard_map/psum | solution.py:77
  9.5 105.0 %copy-start.43 = (pred[384]{0:T(512)(128)(4,1)}, pred[384]{0:T(512)(128)(4,1)S(1)}, u32[]{:S(2)}) copy-start(pred[384]{0:T(512)(128)(4,1)S(1)} %compare_reduce_fusion.1) | copy-start | bytes 1156
  13.8 55.9 %copy-start.10 = (bf16[128,384]{1,0:T(8,128)(2,1)}, bf16[128,384]{1,0:T(8,128)(2,1)S(1)}, u32[]{:S(2)}) copy-start(bf16[128,384]{1,0:T(8,128)(2,1)S(1)} %get-tuple-element.115) | copy-start | bytes 294916
  22.1 92.4 %copy-start.17 = (f32[256,384]{1,0:T(8,128)}, f32[256,384]{1,0:T(8,128)S(1)}, u32[]{:S(2)}) copy-start(f32[256,384]{1,0:T(8,128)S(1)} %get-tuple-element.125) | copy-start | bytes 1179652
  24.1 45.6 %copy-start.56 = (f32[1024]{0:T(1024)S(1)}, f32[1024]{0:T(1024)}, u32[]{:S(2)}) copy-start(f32[1024]{0:T(1024)} %param.32) | copy-start | bytes 12292
  69.7 44.8 %copy-start.47 = (f32[256]{0:T(256)}, f32[256]{0:T(256)S(1)}, u32[]{:S(2)}) copy-start(f32[256]{0:T(256)S(1)} %get-tuple-element.87) | copy-start | bytes 3076
  74.5 284.1 %all-reduce.15.cloned.1.call-start = ((), (), s32[]{:S(2)}) async-start(), calls=%async_computation.1 | async-start | bytes 6422528 | tf_op jit(solution)/shard_map/psum | solution.py:77
  116.6 67.5 %copy-start.35 = (f32[1024]{0:T(1024)S(1)}, f32[1024]{0:T(1024)}, u32[]{:S(2)}) copy-start(f32[1024]{0:T(1024)} %param.33) | copy-start | bytes 12292
  116.6 67.5 %copy-start.44 = (f32[1024]{0:T(1024)S(1)}, f32[1024]{0:T(1024)}, u32[]{:S(2)}) copy-start(f32[1024]{0:T(1024)} %param.34) | copy-start | bytes 12292
  116.6 67.5 %copy-start.59 = (f32[1024]{0:T(1024)S(1)}, f32[1024]{0:T(1024)}, u32[]{:S(2)}) copy-start(f32[1024]{0:T(1024)} %param.36) | copy-start | bytes 12292
  183.8 7.5 %copy-start.2 = (f32[256,1024]{1,0:T(8,128)}, f32[256,1024]{1,0:T(8,128)S(1)}, u32[]{:S(2)}) copy-start(f32[256,1024]{1,0:T(8,128)S(1)} %get-tuple-element.113) | copy-start | bytes 3145732
  184.1 7.2 %copy-start.36 = (f32[256]{0:T(256)}, f32[256]{0:T(256)S(1)}, u32[]{:S(2)}) copy-start(f32[256]{0:T(256)S(1)} %fusion.138) | copy-start | bytes 3076
  199.3 195.0 %all-reduce.19.cloned.1.call-start = ((), (), s32[]{:S(2)}) async-start(), calls=%async_computation.3 | async-start | bytes 12582912 | tf_op jit(solution)/shard_map/psum | solution.py:226
  199.4 5.1 %copy-start.12 = (bf16[128,384]{1,0:T(8,128)(2,1)S(1)}, bf16[128,384]{1,0:T(8,128)(2,1)}, u32[]{:S(2)}) copy-start(bf16[128,384]{1,0:T(8,128)(2,1)} %copy-done.10) | copy-start | bytes 294916
  204.5 99.4 %copy-start.58 = (f32[1024]{0:T(1024)S(1)}, f32[1024]{0:T(1024)}, u32[]{:S(2)}) copy-start(f32[1024]{0:T(1024)} %param.25) | copy-start | bytes 12292
  205.2 98.8 %copy-start.16 = (f32[384,261]{0,1:T(8,128)}, f32[384,261]{0,1:T(8,128)S(1)}, u32[]{:S(2)}) copy-start(f32[384,261]{0,1:T(8,128)S(1)} %get-tuple-element.129) | copy-start | bytes 1202692
  205.3 102.0 %copy-start.37 = (f32[256]{0:T(256)S(1)}, f32[256]{0:T(256)}, u32[]{:S(2)}) copy-start(f32[256]{0:T(256)} %copy-done.36) | copy-start | bytes 3076
  205.4 102.0 %copy-start.45 = (f32[1024]{0:T(1024)S(1)}, f32[1024]{0:T(1024)}, u32[]{:S(2)}) copy-start(f32[1024]{0:T(1024)} %param.34) | copy-start | bytes 12292
  313.7 105.7 %all-reduce.17.cloned.1.call-start = ((), (), s32[]{:S(2)}) async-start(), calls=%async_computation.2 | async-start | bytes 4325376 | tf_op jit(solution)/shard_map/psum | solution.py:210
  (44 other events, 105.7 us)
Sparse Core Ops, SparseCore 0:
  74.6 107.6 all-reduce.12
  199.5 159.1 all-reduce.14
  363.1 31.2 all-reduce.18
  396.7 22.5 all-reduce.16
